TPU v7x, 256 devices: a whole 4x4x8 slice. The times are simulated.
256 devices in a mesh: gx: 8 (over x, core), gy: 4 (over y), gz: 8 (over z).
Axes of the slice: x: 4, y: 4, z: 8, core: 2. Of those that a mesh axis runs over, the one named last changes fastest.
Arguments:
- left_core: float32 [256, 4096, 256], P(None, ('gx', 'gy', 'gz')), may hold values from -4000 to 4000
- right_core: float32 [256, 4096, 256], P(None, ('gx', 'gy', 'gz')), may hold values from -0.00012207031 to 0.00012207031
Outputs:
- left_out: float32 [256, 4096, 128], P(None, ('gx', 'gy', 'gz'))
- right_out: float32 [128, 4096, 256], P(None, ('gx', 'gy', 'gz'))
- next_factor: float32 [256, 256], replicated
All inputs are finite; a program needn't handle non-finite values.
Results may differ from a plain program's by a relative error of at most 0.000075.
Values sent between devices are 32-bit elements; how exact they have to be, the bound alone decides.
A program may use at most 192 MiB of HBM per device.

v0:
```python
import math
import jax
import jax.numpy as jnp
from jax import lax
from jax.sharding import PartitionSpec as P

RK = 128


def gram_of(matrix_rows):
    return lax.dot_general(
        matrix_rows,
        matrix_rows,
        (((0,), (0,)), ((), ())),
        precision=lax.Precision.HIGHEST,
        preferred_element_type=jnp.float32,
    )


def per_device(left_core, right_core):
    rank_left, points_local, rank_mid = left_core.shape
    rank_right = right_core.shape[2]
    total_points = points_local * lax.axis_size("gx") * lax.axis_size("gy") * lax.axis_size("gz")
    unfold = left_core.reshape(rank_left * points_local, rank_mid)
    lower_one = jnp.linalg.cholesky(lax.psum(gram_of(unfold), ("gx", "gy", "gz")))
    upper_full = lower_one.T
    ortho_cols = lax.linalg.triangular_solve(
        lower_one[:RK, :RK], unfold[:, :RK], left_side=False, lower=True, transpose_a=True
    )
    left_out = (ortho_cols * math.sqrt(rank_left * total_points)).reshape(
        rank_left, points_local, RK
    )
    absorbed = jnp.dot(
        upper_full[:RK, :],
        right_core.reshape(rank_mid, points_local * rank_right),
        precision=lax.Precision.HIGHEST,
        preferred_element_type=jnp.float32,
    )
    summed = lax.psum(gram_of(absorbed.reshape(RK * points_local, rank_right)), ("gx", "gy", "gz"))
    factor = jnp.linalg.cholesky(summed / (RK * total_points)).T
    right_out = absorbed.reshape(RK, points_local, rank_right)
    return (left_out, right_out, factor)


def solution(mesh):
    in_specs = (P(None, ("gx", "gy", "gz"), None), P(None, ("gx", "gy", "gz"), None))
    out_specs = (P(None, ("gx", "gy", "gz"), None), P(None, ("gx", "gy", "gz"), None), P())
    return jax.shard_map(
        per_device, mesh=mesh, in_specs=in_specs, out_specs=out_specs, check_vma=False
    )
```

profile of v0, /device:TPU:2, one launch (start us, length us, event | category | flops | bytes accessed | tf_op | source)
XLA Modules:
  0.0 617.6 jit_solution(7845188268302011180)
XLA Ops:
  7.2 0.0 all-reduce.4.cloned.1.call-start
  7.2 10.9 %convolution_bitcast_fusion = f32[256,256]{0,1:T(8,128)} fusion(f32[256,16,256]{2,1,0:T(8,128)} %param.3), kind=kOutput, calls=%fused_computation.3 | convolution fusion | flops 3221225472 | bytes 4456448 | tf_op jit(solution)/shard_map/dot_general | solution.py:11
  18.1 0.0 all-reduce.4.cloned.1.call-update
  18.1 0.5 all-reduce.6.cloned.1.call-start
  18.6 7.9 %copy.26 = f32[32,8,16,256]{3,1,2,0:T(8,128)} copy(f32[32,8,16,256]{3,2,1,0:T(8,128)} %bitcast.53) | data formatting | bytes 8388608
  26.5 244.9 %all-reduce.4.cloned.1.call-done = f32[256,256]{0,1:T(8,128)} async-done(((f32[256,256]{0,1:T(8,128)}), f32[256,256]{0,1:T(8,128)}) %all-reduce.4.cloned.1.call-update) | async-done | bytes 262160 | tf_op jit(solution)/shard_map/psum | solution.py:25
  271.5 1.1 copy.16
  272.6 1.0 fusion.3
  273.6 11.7 %cholesky.130 = f32[128,128]{1,0:T(8,128)S(1)} custom-call(f32[128,128]{1,0:T(8,128)S(1)} %cholesky.194), custom_call_target="Cholesky" | custom-call | tf_op jit(solution)/shard_map/jit(cholesky)/cholesky | solution.py:25
  285.3 9.8 %custom-call.13 = f32[1,128,128]{1,2,0:T(8,128)S(1)} custom-call(f32[1,128,128]{2,1,0:T(8,128)S(1)} %get-tuple-element.17), custom_call_target="InvertDiagBlocksLowerTriangular" | custom-call | tf_op jit(solution)/shard_map/jit(cholesky)/cholesky | solution.py:25
  295.2 0.2 constant_dynamic-update-slice_fusion.3
  295.4 0.3 convolution_subtract_fusion.1
  295.6 11.9 %cholesky.147 = f32[128,128]{1,0:T(8,128)S(1)} custom-call(f32[128,128]{1,0:T(8,128)S(1)} %convolution_subtract_fusion.1), custom_call_target="Cholesky" | custom-call | tf_op jit(solution)/shard_map/jit(cholesky)/cholesky | solution.py:25
  307.5 0.6 compare_reduce_fusion.2
  309.6 4.5 fusion.4
  314.1 1.5 reshape.39
  315.5 6.4 %fusion.14 = f32[256,256]{0,1:T(8,128)} fusion(f32[2048,256]{1,0:T(8,128)} %reshape.39), kind=kOutput, calls=%fused_computation.41 | convolution fusion | flops 1610612736 | bytes 2359296 | tf_op jit(solution)/shard_map/dot_general | solution.py:11
  321.9 0.0 all-reduce.6.cloned.1.call-update
  322.0 9.8 %custom-call.11 = f32[1,128,128]{1,2,0:T(8,128)S(1)} custom-call(f32[1,128,128]{2,1,0:T(8,128)S(1)} %fusion.8), custom_call_target="InvertDiagBlocksLowerTriangular" | custom-call | tf_op jit(solution)/shard_map/triangular_solve | solution.py:27
  331.8 4.9 fusion
  336.7 2.0 copy.27
  338.6 3.1 copy.17
  341.7 229.4 %all-reduce.6.cloned.1.call-done = f32[256,256]{0,1:T(8,128)} async-done(((f32[256,256]{0,1:T(8,128)}), f32[256,256]{0,1:T(8,128)}) %all-reduce.6.cloned.1.call-update) | async-done | bytes 262160 | tf_op jit(solution)/shard_map/psum | solution.py:39
  571.1 1.0 broadcast_multiply_fusion
  572.0 0.1 copy.19
  572.2 1.0 fusion.2
  573.2 11.7 %cholesky.164 = f32[128,128]{1,0:T(8,128)S(1)} custom-call(f32[128,128]{1,0:T(8,128)S(1)} %cholesky.197), custom_call_target="Cholesky" | custom-call | tf_op jit(solution)/shard_map/jit(cholesky)/cholesky | solution.py:40
  585.0 9.8 %custom-call.14 = f32[1,128,128]{1,2,0:T(8,128)S(1)} custom-call(f32[1,128,128]{2,1,0:T(8,128)S(1)} %get-tuple-element.13), custom_call_target="InvertDiagBlocksLowerTriangular" | custom-call | tf_op jit(solution)/shard_map/jit(cholesky)/cholesky | solution.py:40
  594.8 0.2 constant_dynamic-update-slice_fusion.1
  595.0 0.3 convolution_subtract_fusion
  595.3 11.7 %cholesky.181 = f32[128,128]{1,0:T(8,128)S(1)} custom-call(f32[128,128]{1,0:T(8,128)S(1)} %convolution_subtract_fusion), custom_call_target="Cholesky" | custom-call | tf_op jit(solution)/shard_map/jit(cholesky)/cholesky | solution.py:40
  607.0 0.7 compare_reduce_fusion
  607.7 0.6 compare_reduce_fusion.1
  609.7 0.8 copy.20
  (12 shorter events, 0.3 us)
Async XLA Ops:
  7.2 264.3 %all-reduce.4.cloned.1.call-start = ((), (), s32[]{:S(2)}) async-start(), calls=%async_computation | async-start | bytes 524288 | tf_op jit(solution)/shard_map/psum | solution.py:25
  18.1 552.9 %all-reduce.6.cloned.1.call-start = ((), (), s32[]{:S(2)}) async-start(), calls=%async_computation.1 | async-start | bytes 524288 | tf_op jit(solution)/shard_map/psum | solution.py:39
Sparse Core Ops, SparseCore 0:
  18.2 253.1 all-reduce.3
  322.1 248.9 all-reduce.5
where the time goes:
time: 623 us; the launch traced here: 618 us
  waiting for transfers between devices  474 us (76%)
  other arithmetic  81.6 us (13%)
  matrix products  27.6 us (4%)
  between operations  17.1 us (3%)
  local copies, waits for them, and re-layouts  16.5 us (3%)
    psum x1, waiting for transfers between devices, per_device(): lax.psum(gram_of(unfold), ('gx', 'gy', 'gz'))  245 us
    psum x1, waiting for transfers between devices, per_device(): lax.psum(gram_of(absorbed.reshape(RK * points_local, rank_right)), ('gx',...  229 us
    another operation x7, other arithmetic, per_device(): factor = jnp.linalg.cholesky(summed / (RK * total_points)).T  34.7 us
    another operation x6, other arithmetic, per_device(): jnp.linalg.cholesky(lax.psum(gram_of(unfold), ('gx', 'gy', 'gz')))  34.1 us
    dot_general x2, matrix products, gram_of(): lax.dot_general(matrix_rows, matrix_rows, (((0,), (0,)), ((), ())), preci...  17.3 us
  transfers between devices with their start and end apart: 2, of which 2 were waited for; matrix products, arithmetic and copies ran while one was open for 4% of the time, Pallas kernels for 0%

commit v1 on v0

--- a/solution.py
+++ b/solution.py
@@ -36,7 +36,9 @@
         precision=lax.Precision.HIGHEST,
         preferred_element_type=jnp.float32,
     )
-    summed = lax.psum(gram_of(absorbed.reshape(RK * points_local, rank_right)), ("gx", "gy", "gz"))
+    summed = lax.psum(
+        lax.psum(gram_of(absorbed.reshape(RK * points_local, rank_right)), "gx"), ("gy", "gz")
+    )
     factor = jnp.linalg.cholesky(summed / (RK * total_points)).T
     right_out = absorbed.reshape(RK, points_local, rank_right)
     return (left_out, right_out, factor)

time: 623 us -> 585 us (0.939)
  waiting for transfers between devices: 474 us -> 439 us
    psum x1 -> x2, waiting for transfers between devices: 229 us -> 194 us  [the longest x1 144 us: per_device(): lax.psum(lax.psum(gram_of(absorbed.reshape(RK * points_local, rank_right)...]
  transfers between devices with their start and end apart: 2 -> 3, of which waited for: 2 -> 3; matrix products, arithmetic and copies ran while one was open for 4% -> 4% of each run, Pallas kernels for 0% -> 0%
where the time goes in v1:
time: 585 us; the launch traced here: 579 us
  waiting for transfers between devices  439 us (75%)
  other arithmetic  81.6 us (14%)
  matrix products  26.2 us (4%)
  between operations  16.8 us (3%)
  local copies, waits for them, and re-layouts  15.5 us (3%)
    psum x1, waiting for transfers between devices, per_device(): lax.psum(gram_of(unfold), ('gx', 'gy', 'gz'))  245 us
    psum x1, waiting for transfers between devices, per_device(): lax.psum(lax.psum(gram_of(absorbed.reshape(RK * points_local, rank_right)...  144 us
    psum x1, waiting for transfers between devices, per_device(): lax.psum(gram_of(absorbed.reshape(RK * points_local, rank_right)), 'gx')  49.7 us
    another operation x7, other arithmetic, per_device(): factor = jnp.linalg.cholesky(summed / (RK * total_points)).T  34.7 us
    another operation x6, other arithmetic, per_device(): jnp.linalg.cholesky(lax.psum(gram_of(unfold), ('gx', 'gy', 'gz')))  34.1 us
    dot_general x2, matrix products, gram_of(): lax.dot_general(matrix_rows, matrix_rows, (((0,), (0,)), ((), ())), preci...  17.3 us
  transfers between devices with their start and end apart: 3, of which 3 were waited for; matrix products, arithmetic and copies ran while one was open for 4% of the time, Pallas kernels for 0%

profile of v1, /device:TPU:2, one launch (start us, length us, event | category | flops | bytes accessed | tf_op | source)
XLA Modules:
  0.0 579.2 jit_solution(320095401093729599)
XLA Ops:
  7.2 0.0 all-reduce.5.cloned.1.call-start
  7.2 10.9 %convolution_bitcast_fusion = f32[256,256]{0,1:T(8,128)} fusion(f32[256,16,256]{2,1,0:T(8,128)} %param.3), kind=kOutput, calls=%fused_computation.3 | convolution fusion | flops 3221225472 | bytes 4456448 | tf_op jit(solution)/shard_map/dot_general | solution.py:11
  18.1 0.0 all-reduce.5.cloned.1.call-update
  18.1 0.5 all-reduce.7.cloned.1.call-start
  18.6 7.9 %copy.26 = f32[32,8,16,256]{3,1,2,0:T(8,128)} copy(f32[32,8,16,256]{3,2,1,0:T(8,128)} %bitcast.53) | data formatting | bytes 8388608
  26.5 244.9 %all-reduce.5.cloned.1.call-done = f32[256,256]{0,1:T(8,128)} async-done(((f32[256,256]{0,1:T(8,128)}), f32[256,256]{0,1:T(8,128)}) %all-reduce.5.cloned.1.call-update) | async-done | bytes 262160 | tf_op jit(solution)/shard_map/psum | solution.py:25
  271.5 1.1 copy.16
  272.6 1.0 fusion.3
  273.6 11.7 %cholesky.130 = f32[128,128]{1,0:T(8,128)S(1)} custom-call(f32[128,128]{1,0:T(8,128)S(1)} %cholesky.194), custom_call_target="Cholesky" | custom-call | tf_op jit(solution)/shard_map/jit(cholesky)/cholesky | solution.py:25
  285.3 9.8 %custom-call.13 = f32[1,128,128]{1,2,0:T(8,128)S(1)} custom-call(f32[1,128,128]{2,1,0:T(8,128)S(1)} %get-tuple-element.17), custom_call_target="InvertDiagBlocksLowerTriangular" | custom-call | tf_op jit(solution)/shard_map/jit(cholesky)/cholesky | solution.py:25
  295.2 0.2 constant_dynamic-update-slice_fusion.3
  295.4 0.3 convolution_subtract_fusion.1
  295.6 11.9 %cholesky.147 = f32[128,128]{1,0:T(8,128)S(1)} custom-call(f32[128,128]{1,0:T(8,128)S(1)} %convolution_subtract_fusion.1), custom_call_target="Cholesky" | custom-call | tf_op jit(solution)/shard_map/jit(cholesky)/cholesky | solution.py:25
  307.5 0.6 compare_reduce_fusion.2
  309.6 4.5 fusion.4
  314.1 1.5 reshape.39
  315.5 6.4 %fusion.14 = f32[256,256]{0,1:T(8,128)} fusion(f32[2048,256]{1,0:T(8,128)} %reshape.39), kind=kOutput, calls=%fused_computation.41 | convolution fusion | flops 1610612736 | bytes 2359296 | tf_op jit(solution)/shard_map/dot_general | solution.py:11
  321.9 0.0 all-reduce.7.cloned.1.call-update
  321.9 0.0 all-reduce.9.cloned.1.call-start
  322.0 2.0 copy.27
  324.0 9.8 %custom-call.11 = f32[1,128,128]{1,2,0:T(8,128)S(1)} custom-call(f32[1,128,128]{2,1,0:T(8,128)S(1)} %fusion.8), custom_call_target="InvertDiagBlocksLowerTriangular" | custom-call | tf_op jit(solution)/shard_map/triangular_solve | solution.py:27
  333.8 49.7 %all-reduce.7.cloned.1.call-done = f32[256,256]{0,1:T(8,128)} async-done(((f32[256,256]{0,1:T(8,128)}), f32[256,256]{0,1:T(8,128)}) %all-reduce.7.cloned.1.call-update) | async-done | bytes 262160 | tf_op jit(solution)/shard_map/psum | solution.py:40
  383.5 0.0 all-reduce.9.cloned.1.call-update
  383.5 3.5 fusion
  387.0 2.0 copy.17
  389.1 143.9 %all-reduce.9.cloned.1.call-done = f32[256,256]{0,1:T(8,128)} async-done(((f32[256,256]{0,1:T(8,128)}), f32[256,256]{0,1:T(8,128)}) %all-reduce.9.cloned.1.call-update) | async-done | bytes 262160 | tf_op jit(solution)/shard_map/psum | solution.py:39
  532.9 1.0 broadcast_multiply_fusion
  533.9 0.1 copy.19
  534.0 1.0 fusion.2
  535.1 11.7 %cholesky.164 = f32[128,128]{1,0:T(8,128)S(1)} custom-call(f32[128,128]{1,0:T(8,128)S(1)} %cholesky.197), custom_call_target="Cholesky" | custom-call | tf_op jit(solution)/shard_map/jit(cholesky)/cholesky | solution.py:42
  546.8 9.8 %custom-call.14 = f32[1,128,128]{1,2,0:T(8,128)S(1)} custom-call(f32[1,128,128]{2,1,0:T(8,128)S(1)} %get-tuple-element.13), custom_call_target="InvertDiagBlocksLowerTriangular" | custom-call | tf_op jit(solution)/shard_map/jit(cholesky)/cholesky | solution.py:42
  556.6 0.2 constant_dynamic-update-slice_fusion.1
  556.9 0.3 convolution_subtract_fusion
  557.1 11.7 %cholesky.181 = f32[128,128]{1,0:T(8,128)S(1)} custom-call(f32[128,128]{1,0:T(8,128)S(1)} %convolution_subtract_fusion), custom_call_target="Cholesky" | custom-call | tf_op jit(solution)/shard_map/jit(cholesky)/cholesky | solution.py:42
  568.9 0.7 compare_reduce_fusion
  569.6 0.6 compare_reduce_fusion.1
  571.6 0.8 copy.20
  (12 shorter events, 0.3 us)
Async XLA Ops:
  7.2 264.3 %all-reduce.5.cloned.1.call-start = ((), (), s32[]{:S(2)}) async-start(), calls=%async_computation | async-start | bytes 524288 | tf_op jit(solution)/shard_map/psum | solution.py:25
  18.1 365.4 %all-reduce.7.cloned.1.call-start = ((), (), s32[]{:S(2)}) async-start(), calls=%async_computation.1 | async-start | bytes 524288 | tf_op jit(solution)/shard_map/psum | solution.py:40
  321.9 211.0 %all-reduce.9.cloned.1.call-start = ((), (), s32[]{:S(2)}) async-start(), calls=%async_computation.2 | async-start | bytes 524288 | tf_op jit(solution)/shard_map/psum | solution.py:39
Sparse Core Ops, SparseCore 0:
  18.2 253.1 all-reduce.4
  322.1 61.3 all-reduce.6
  387.4 145.5 all-reduce.8
